TPU v7x, 32 devices: a whole 2x2x4 slice. The times are simulated.
32 devices in a mesh: cells: 8 (over z, x), seq: 4 (over y, core).
Axes of the slice: x: 2, y: 2, z: 4, core: 2. Of those that a mesh axis runs over, the one named last changes fastest.
Arguments:
- cell_tokens: bfloat16 [8, 1280, 1120], P('cells', 'seq'), may hold values from -6 to 6
- drop_counts: int32 [8], P('cells'), may hold values from 0 to 4, as said below
- lengths: int32 [8], P('cells'), may hold values from 640 to 1280, as said below
- ln_gain: bfloat16 [2, 1120], replicated, may hold values from 0.25 to 1.75
- ln_shift: bfloat16 [2, 1120], replicated, may hold values from -1.1953125 to 1.1953125
- w_qkv: bfloat16 [3, 1120, 1120], P(None, None, 'seq'), may hold values from -0.1875 to 0.1875
- qv_bias: bfloat16 [2, 1120], P(None, 'seq'), may hold values from -0.29882812 to 0.29882812
- w_out: bfloat16 [1120, 1120], P('seq'), may hold values from -1.5 to 1.5
- out_bias: bfloat16 [2, 1120], replicated, may hold values from -1.1953125 to 1.1953125
- w_up: bfloat16 [4480, 1120], P('cells', 'seq'), may hold values from -0.1875 to 0.1875
- up_bias: bfloat16 [4480], replicated, may hold values from -1.1953125 to 1.1953125
- w_down: bfloat16 [4480, 1120], P('cells', 'seq'), may hold values from -0.09375 to 0.09375
- out_grad: bfloat16 [8, 1280, 1120], P('cells', 'seq'), may hold values from -6 to 6
Outputs:
- block_out: bfloat16 [8, 1280, 1120], P('cells', 'seq')
- in_grad: float32 [8, 1280, 1120], P('cells', 'seq')
- d_ln_gain: float32 [2, 1120], replicated
- d_ln_shift: float32 [2, 1120], replicated
- d_qkv: float32 [3, 1120, 1120], P(None, None, 'seq')
- d_qv_bias: float32 [2, 1120], P(None, 'seq')
- d_out: float32 [1120, 1120], P('seq')
- d_out_bias: float32 [2, 1120], replicated
- d_up: float32 [4480, 1120], P('cells', 'seq')
- d_up_bias: float32 [4480], replicated
- d_down: float32 [4480, 1120], P('cells', 'seq')
Inputs may be any that keep to these rules, and one draw needn't show every extreme that they name: `drop_counts`: one sentence in every draw masks its first 4 positions as keys and one masks none. `lengths`: in every draw one sentence is 1280 long and one is 640 long.
All inputs are finite; a program needn't handle non-finite values.
Results may differ from a plain program's by a relative error of at most 0.012.
The roundings to bfloat16 on the way count: a program that leaves them out, or rounds other values in their place, can miss the bound.
Values may be sent and summed in bfloat16 or wider, within the bound.
A program may use at most 256 MiB of HBM per device.

v0:
```python
import math
import jax
import jax.numpy as jnp
from jax import lax
from jax.sharding import PartitionSpec as P

HEADS = 20
HD = 56
QBLOCK = 640
epsilon = 1e-05
masked_score = -1e30


def layer_norm(rows, gain, shift):
    centre = jnp.mean(rows, axis=-1, keepdims=True)
    offsets = rows - centre
    spread = jnp.mean(offsets * offsets, axis=-1, keepdims=True)
    return offsets * lax.rsqrt(spread + epsilon) * gain + shift


def gelu_tanh(values):
    return jax.nn.gelu(values, approximate=True)


def visible(drop_counts, lengths, start_row, row_count, key_count):
    query_place = start_row + jnp.arange(row_count, dtype=jnp.int32)[:, None]
    key_place = jnp.arange(key_count, dtype=jnp.int32)[None, :]
    dropped = drop_counts[:, None, None, None]
    limits = lengths[:, None, None, None]
    return (
        (key_place <= query_place)
        & (key_place < limits)
        & ((key_place >= dropped) | (key_place == query_place))
    )


def attend(packed, drop_counts, lengths, scale):
    queries = packed[:, :, :, 0]
    keys_all = packed[:, :, :, 1]
    values = packed[:, :, :, 2]
    outputs = []
    log_sums = []
    for start_row in range(0, queries.shape[1], QBLOCK):
        end_row = start_row + QBLOCK
        scores = (
            jnp.einsum(
                "cqhe,ckhe->chqk",
                queries[:, start_row:end_row],
                keys_all[:, :end_row],
                preferred_element_type=jnp.float32,
            )
            * scale
        )
        allowed = visible(drop_counts, lengths, start_row, QBLOCK, end_row)
        scores = jnp.where(allowed, scores, masked_score)
        largest = jnp.max(scores, axis=-1, keepdims=True)
        weights = jnp.where(allowed, jnp.exp(scores - largest), 0.0)
        totals = jnp.sum(weights, axis=-1, keepdims=True)
        probs = (weights / totals).astype(jnp.bfloat16)
        piece_out = jnp.einsum(
            "chqk,ckhe->cqhe", probs, values[:, :end_row], preferred_element_type=jnp.float32
        )
        outputs.append(piece_out.astype(jnp.bfloat16))
        log_sums.append(jnp.transpose((largest + jnp.log(totals))[..., 0], (0, 2, 1)))
    return (jnp.concatenate(outputs, axis=1), jnp.concatenate(log_sums, axis=1))


def attend_back(packed, grad_out, log_sums, drop_counts, lengths, scale):
    queries = packed[:, :, :, 0]
    keys_all = packed[:, :, :, 1]
    values = packed[:, :, :, 2]
    grad_query = []
    grad_key = jnp.zeros(keys_all.shape, jnp.float32)
    grad_value = jnp.zeros(values.shape, jnp.float32)
    for start_row in range(0, queries.shape[1], QBLOCK):
        end_row = start_row + QBLOCK
        scores = (
            jnp.einsum(
                "cqhe,ckhe->chqk",
                queries[:, start_row:end_row],
                keys_all[:, :end_row],
                preferred_element_type=jnp.float32,
            )
            * scale
        )
        allowed = visible(drop_counts, lengths, start_row, QBLOCK, end_row)
        block_sums = jnp.transpose(log_sums[:, start_row:end_row], (0, 2, 1))[..., None]
        probs = jnp.where(
            allowed, jnp.exp(jnp.where(allowed, scores, masked_score) - block_sums), 0.0
        )
        grad_rows = grad_out[:, start_row:end_row]
        grad_probs = jnp.einsum(
            "cqhe,ckhe->chqk", grad_rows, values[:, :end_row], preferred_element_type=jnp.float32
        )
        centre = jnp.sum(probs * grad_probs, axis=-1, keepdims=True)
        grad_scores = (probs * (grad_probs - centre) * scale).astype(jnp.bfloat16)
        grad_query.append(
            jnp.einsum(
                "chqk,ckhe->cqhe",
                grad_scores,
                keys_all[:, :end_row],
                preferred_element_type=jnp.float32,
            ).astype(jnp.bfloat16)
        )
        grad_key = grad_key.at[:, :end_row].add(
            jnp.einsum(
                "chqk,cqhe->ckhe",
                grad_scores,
                queries[:, start_row:end_row],
                preferred_element_type=jnp.float32,
            )
        )
        grad_value = grad_value.at[:, :end_row].add(
            jnp.einsum(
                "chqk,cqhe->ckhe",
                probs.astype(jnp.bfloat16),
                grad_rows,
                preferred_element_type=jnp.float32,
            )
        )
    return jnp.stack(
        [
            jnp.concatenate(grad_query, axis=1),
            grad_key.astype(jnp.bfloat16),
            grad_value.astype(jnp.bfloat16),
        ],
        axis=3,
    )


def head_bias(pair_bias, head_count):
    stacked = jnp.stack([pair_bias[0], jnp.zeros_like(pair_bias[0]), pair_bias[1]]).astype(
        jnp.float32
    )
    return jnp.transpose(stacked.reshape(3, head_count, HD), (1, 0, 2))


def bias_grads(grad_packed):
    summed = jnp.sum(grad_packed, axis=(0, 1), dtype=jnp.float32)
    return jnp.stack([summed[:, 0].reshape(-1), summed[:, 2].reshape(-1)])


def body(
    cell_tokens,
    drop_counts,
    lengths,
    ln_gain,
    ln_shift,
    w_qkv,
    qv_bias,
    w_out,
    out_bias,
    w_up,
    up_bias,
    w_down,
    out_grad,
):
    scale = 1.0 / math.sqrt(HD)
    up_rows, down_rows = (
        lax.all_gather(w_up, "cells", axis=0, tiled=True),
        lax.all_gather(w_down, "cells", axis=0, tiled=True),
    )
    up_unit, down_unit = (
        lax.all_to_all(up_rows, "seq", split_axis=0, concat_axis=1, tiled=True),
        lax.all_to_all(down_rows, "seq", split_axis=0, concat_axis=1, tiled=True),
    )
    gains = ln_gain.astype(jnp.float32)
    shifts = ln_shift.astype(jnp.float32)
    biases = out_bias.astype(jnp.float32)
    tokens = cell_tokens.astype(jnp.float32)
    cells_here, rows_here, width = tokens.shape
    normed_f, norm_back = jax.vjp(layer_norm, tokens, gains[0], shifts[0])
    normed = normed_f.astype(jnp.bfloat16)
    qkv_full, out_full, bias_full = (
        lax.all_gather(w_qkv, "seq", axis=2, tiled=True),
        lax.all_gather(w_out, "seq", axis=0, tiled=True),
        lax.all_gather(qv_bias, "seq", axis=1, tiled=True),
    )
    qkv_heads = qkv_full.reshape(3, width, HEADS, HD)
    packed = jnp.einsum(
        "csd,tdhe->cshte", normed, qkv_heads, preferred_element_type=jnp.float32
    ) + head_bias(bias_full, HEADS)
    packed = packed.astype(jnp.bfloat16)
    group_count = lax.axis_size("seq")
    grouped = packed.reshape(cells_here, rows_here, group_count, HEADS // group_count, 3, HD)
    moved_heads = lax.all_to_all(grouped, "seq", split_axis=2, concat_axis=1, tiled=True)[:, :, 0]
    head_out, log_sums = attend(moved_heads, drop_counts, lengths, scale)
    head_out, log_sums, moved_kept = (head_out, log_sums, moved_heads)
    mixed = lax.all_to_all(head_out, "seq", split_axis=1, concat_axis=2, tiled=True).reshape(
        cells_here, rows_here, width
    )
    branch = (
        jnp.einsum("csd,de->cse", mixed, out_full, preferred_element_type=jnp.float32) + biases[0]
    )
    middle = tokens + branch
    normed2_f, norm_back2 = jax.vjp(layer_norm, middle, gains[1], shifts[1])
    normed2 = normed2_f.astype(jnp.bfloat16)
    normed2_all, grad_all = (
        lax.all_gather(normed2, "seq", axis=1, tiled=True),
        lax.all_gather(out_grad, "seq", axis=1, tiled=True),
    )
    units = up_unit.shape[0]
    first_unit = lax.axis_index("seq") * units
    bias_unit = lax.dynamic_slice_in_dim(up_bias, first_unit, units).astype(jnp.float32)
    hidden = (
        jnp.einsum("csd,fd->csf", normed2_all, up_unit, preferred_element_type=jnp.float32)
        + bias_unit
    )
    active_f, gelu_back = jax.vjp(gelu_tanh, hidden)
    active = active_f.astype(jnp.bfloat16)
    down_terms = jnp.einsum("csf,fd->csd", active, down_unit, preferred_element_type=jnp.float32)
    branch2 = (
        lax.psum_scatter(
            down_terms.astype(jnp.bfloat16), "seq", scatter_dimension=1, tiled=True
        ).astype(jnp.float32)
        + biases[1]
    )
    block_out = (middle + branch2).astype(jnp.bfloat16)
    grad_down_unit = jnp.einsum("csf,csd->fd", active, grad_all, preferred_element_type=jnp.float32)
    grad_active = jnp.einsum("csd,fd->csf", grad_all, down_unit, preferred_element_type=jnp.float32)
    grad_hidden = gelu_back(grad_active)[0].astype(jnp.bfloat16)
    grad_up_unit = jnp.einsum(
        "csf,csd->fd", grad_hidden, normed2_all, preferred_element_type=jnp.float32
    )
    unit_bias_grad = jnp.sum(grad_hidden, axis=(0, 1), dtype=jnp.float32)
    grad_up_bias = lax.dynamic_update_slice_in_dim(
        jnp.zeros((up_bias.shape[0],), jnp.float32), unit_bias_grad, first_unit, 0
    )
    normed2_terms = jnp.einsum(
        "csf,fd->csd", grad_hidden, up_unit, preferred_element_type=jnp.float32
    )
    grad_normed2 = lax.psum_scatter(normed2_terms, "seq", scatter_dimension=1, tiled=True)
    up_part, down_part = (
        lax.all_to_all(grad_up_unit, "seq", split_axis=1, concat_axis=0, tiled=True),
        lax.all_to_all(grad_down_unit, "seq", split_axis=1, concat_axis=0, tiled=True),
    )
    grad_middle_norm, grad_gain2, grad_shift2 = norm_back2(grad_normed2)
    grad_middle = out_grad.astype(jnp.float32) + grad_middle_norm
    grad_branch = grad_middle.astype(jnp.bfloat16)
    grad_bias_attn = jnp.sum(grad_branch, axis=(0, 1), dtype=jnp.float32)
    grad_bias_down = jnp.sum(out_grad, axis=(0, 1), dtype=jnp.float32)
    d_up, d_down = (
        lax.psum_scatter(up_part, "cells", scatter_dimension=0, tiled=True),
        lax.psum_scatter(down_part, "cells", scatter_dimension=0, tiled=True),
    )
    grad_out_w = jnp.einsum("csd,cse->de", mixed, grad_branch, preferred_element_type=jnp.float32)
    grad_mixed = jnp.einsum(
        "cse,de->csd", grad_branch, out_full, preferred_element_type=jnp.float32
    ).astype(jnp.bfloat16)
    grad_mixed = grad_mixed.reshape(cells_here, rows_here, HEADS, HD)
    grad_heads = lax.all_to_all(grad_mixed, "seq", split_axis=2, concat_axis=1, tiled=True)
    grad_packed_heads = attend_back(moved_kept, grad_heads, log_sums, drop_counts, lengths, scale)
    grad_packed = lax.all_to_all(grad_packed_heads, "seq", split_axis=1, concat_axis=2, tiled=True)
    grad_qkv_full = jnp.einsum(
        "csd,cshte->tdhe", normed, grad_packed, preferred_element_type=jnp.float32
    ).reshape(3, width, width)
    grad_normed = jnp.einsum(
        "cshte,tdhe->csd", grad_packed, qkv_heads, preferred_element_type=jnp.float32
    )
    grad_qkv_own, grad_bias_own, grad_out_own = (
        lax.psum_scatter(grad_qkv_full, "seq", scatter_dimension=2, tiled=True),
        lax.psum_scatter(bias_grads(grad_packed), "seq", scatter_dimension=1, tiled=True),
        lax.psum_scatter(grad_out_w, "seq", scatter_dimension=0, tiled=True),
    )
    d_qkv, d_qv_bias, d_out = lax.psum((grad_qkv_own, grad_bias_own, grad_out_own), "cells")
    grad_tokens_norm, grad_gain1, grad_shift1 = norm_back(grad_normed)
    in_grad = grad_middle + grad_tokens_norm
    d_ln_gain, d_ln_shift, d_out_bias, d_up_bias = lax.psum(
        (
            jnp.stack([grad_gain1, grad_gain2]),
            jnp.stack([grad_shift1, grad_shift2]),
            jnp.stack([grad_bias_attn, grad_bias_down]),
            grad_up_bias,
        ),
        ("cells", "seq"),
    )
    return (
        block_out,
        in_grad,
        d_ln_gain,
        d_ln_shift,
        d_qkv,
        d_qv_bias,
        d_out,
        d_out_bias,
        d_up,
        d_up_bias,
        d_down,
    )


def solution(mesh):
    placed = (
        P("cells", "seq", None),
        P("cells"),
        P("cells"),
        P(),
        P(),
        P(None, None, "seq"),
        P(None, "seq"),
        P("seq", None),
        P(),
        P("cells", "seq"),
        P(),
        P("cells", "seq"),
        P("cells", "seq", None),
    )
    return jax.shard_map(
        body,
        mesh=mesh,
        in_specs=placed,
        out_specs=(
            P("cells", "seq", None),
            P("cells", "seq", None),
            P(),
            P(),
            P(None, None, "seq"),
            P(None, "seq"),
            P("seq", None),
            P(),
            P("cells", "seq"),
            P(),
            P("cells", "seq"),
        ),
        check_vma=False,
    )
```

profile of v0, /device:TPU:0, one launch (start us, length us, event | category | flops | bytes accessed | tf_op | source)
XLA Modules:
  0.0 1321.3 jit_solution(9016403108067090573)
XLA Ops:
  9.4 6.3 all-gather
  21.2 45.7 %all-gather.10.cloned.1.call-done = bf16[3,1120,1120]{1,2,0:T(8,128)(2,1)} async-done(((bf16[3,1120,280]{1,2,0:T(8,128)(2,1)}), bf16[3,1120,1120]{1,2,0:T(8,128)(2,1)}) %all-gather.10.cloned.1.call-update) | async-done | bytes 7526416 | tf_op jit(solution)/shard_map/all_gather | solution.py:175
  66.9 7.4 fusion.135
  76.8 3.7 all-to-all-start
  84.5 35.4 %all-to-all-done = bf16[1,320,4,5,3,56]{1,5,3,4,0,2:T(8,128)(2,1)S(1)} async-done(((bf16[1,320,4,5,3,56]{1,5,3,4,0,2:T(8,128)(2,1)}), bf16[1,320,4,5,3,56]{1,5,3,4,0,2:T(8,128)(2,1)S(1)}, u32[]{:S(2)}, u32[]{:S(2)}) %all-to-all-start) | async-done | bytes 2150432 | tf_op jit(solution)/shard_map/all_to_all | solution.py:186
  122.4 4.5 squeeze.15
  127.1 9.1 fusion.181
  143.2 9.6 fusion.6
  152.9 9.2 fusion.122
  165.0 3.8 reshape.827
  168.8 4.2 all-to-all-start.1
  173.1 10.9 all-to-all-done.1
  184.0 4.4 reshape.828
  191.0 3.7 fusion.182
  196.9 3.8 copy.92
  200.7 6.0 all_to_all.104
  206.7 3.5 copy.93
  210.2 4.5 all-to-all-start.2
  214.8 6.1 all-gather.20.cloned.1.call-done
  220.8 3.7 copy.94
  224.6 6.1 all_to_all.108
  230.7 3.5 copy.95
  234.2 25.9 %all-to-all-done.2 = bf16[4,1120,280]{1,2,0:T(8,128)(2,1)} async-done(((bf16[4,1120,280]{1,2,0:T(8,128)(2,1)}), bf16[4,1120,280]{1,2,0:T(8,128)(2,1)}, u32[]{:S(2)}, u32[]{:S(2)}) %all-to-all-start.2) | async-done | bytes 2508832 | tf_op jit(solution)/shard_map/all_to_all | solution.py:164
  260.1 4.6 all-to-all-start.3
  265.5 9.1 convolution_add_fusion
  274.6 33.1 %all-gather.16.cloned.1.call-done = bf16[1,1280,1120]{2,1,0:T(8,128)(2,1)} async-done(((bf16[1,320,1120]{2,1,0:T(8,128)(2,1)}), bf16[1,1280,1120]{2,1,0:T(8,128)(2,1)}) %all-gather.16.cloned.1.call-update) | async-done | bytes 2867216 | tf_op jit(solution)/shard_map/all_gather | solution.py:200
  307.7 3.8 all-to-all-done.3
  311.4 12.8 convert_reduce_fusion
  325.8 8.1 convolution_bitcast_fusion.1
  333.9 10.4 fusion.36
  344.4 45.2 %reduce-scatter.16.cloned.1.call-done = f32[1,320,1120]{2,1,0:T(8,128)} async-done(((f32[1,1280,1120]{2,1,0:T(8,128)}), f32[1,320,1120]{2,1,0:T(8,128)}) %reduce-scatter.16.cloned.1.call-update) | async-done | bytes 1433616 | tf_op jit(solution)/shard_map/reduce_scatter | solution.py:232
  391.5 38.1 %reduce-scatter.14.cloned.1.call-done = bf16[1,320,1120]{2,1,0:T(8,128)(2,1)} async-done(((bf16[1,1280,1120]{2,1,0:T(8,128)(2,1)}), bf16[1,320,1120]{2,1,0:T(8,128)(2,1)}) %reduce-scatter.14.cloned.1.call-update) | async-done | bytes 716816 | tf_op jit(solution)/shard_map/reduce_scatter | solution.py:213
  434.1 3.9 fusion.132
  446.1 12.2 all-to-all-done.4
  459.3 5.7 fusion.146
  465.0 17.3 %fusion.123 = bf16[1,640,5,56]{1,3,2,0:T(8,128)(2,1)} fusion(f32[5,640,640]{1,2,0:T(8,128)} %fusion.146, bf16[1,1280,5,56]{1,3,2,0:T(8,128)(2,1)S(1)} %copy-done.19, f32[5,640,640]{1,2,0:T(8,128)} %copy-done.7, f32[5,640]{1,0:T(8,128)S(1)} %log_add_fusion.1, pred[640,640]{0,1:T(8,128)(4,1)S(1)} %copy-done.14), kind=kOutput, calls=%fused_computation.124 | convolution fusion | flops 256183040 | bytes 34344960 | tf_op jit(solution)/shard_map/chqk,ckhe->cqhe/dot_general | solution.py:98
  482.3 17.6 %fusion.111 = f32[1,640,5,56]{1,3,2,0:T(8,128)} fusion(f32[5,640,640]{1,2,0:T(8,128)} %fusion.146, bf16[1,1280,5,56]{1,3,2,0:T(8,128)(2,1)} %copy-done.15, f32[5,640,640]{1,2,0:T(8,128)} %copy-done.7, f32[5,640]{1,0:T(8,128)S(1)} %log_add_fusion.1, pred[640,640]{0,1:T(8,128)(4,1)S(1)} %copy-done.14), kind=kOutput, calls=%fused_computation.118 | convolution fusion | flops 256003840 | bytes 34703360 | tf_op jit(solution)/shard_map/chqk,cqhe->ckhe/dot_general | solution.py:106
  499.9 9.0 fusion.139
  508.9 35.1 %fusion.91 = bf16[1,1280,5,1,56]{1,4,2,3,0:T(8,128)(2,1)} fusion(f32[5,640,1280]{2,1,0:T(8,128)} %fusion.139, f32[5,640,1280]{2,1,0:T(8,128)} %get-tuple-element.107, f32[5,640]{1,0:T(8,128)S(1)} %log_add_fusion, pred[640,1280]{1,0:T(8,128)(4,1)} %fusion.57, f32[1,640,5,56]{1,3,2,0:T(8,128)} %fusion.111, bf16[1,1280,5,56]{1,3,2,0:T(8,128)(2,1)} %copy-done.15), kind=kOutput, calls=%fused_computation.84 | convolution fusion | flops 496337280 | bytes 69007360 | tf_op jit(solution)/shard_map/chqk,cqhe->ckhe/dot_general | solution.py:106
  544.0 33.6 %fusion.127 = bf16[1,640,5,56]{1,3,2,0:T(8,128)(2,1)} fusion(f32[5,640,1280]{2,1,0:T(8,128)} %fusion.139, f32[5,640,1280]{2,1,0:T(8,128)} %get-tuple-element.107, f32[5,640]{1,0:T(8,128)S(1)} %log_add_fusion, pred[640,1280]{1,0:T(8,128)(4,1)} %fusion.57, bf16[1,1280,5,3,56]{1,4,2,3,0:T(8,128)(2,1)S(1)} %copy-done.2), kind=kOutput, calls=%fused_computation.126 | convolution fusion | flops 495799680 | bytes 68290560 | tf_op jit(solution)/shard_map/chqk,ckhe->cqhe/dot_general | solution.py:98
  578.8 6.0 fusion.108
  584.9 8.4 fusion.88
  593.5 6.3 copy.104
  599.8 10.7 reshape.829
  610.5 29.5 %all_to_all.133 = bf16[4,2,134400]{2,1,0:T(2,128)(2,1)} all-to-all(bf16[4,2,134400]{2,1,0:T(2,128)(2,1)S(1)} %reshape.829), channel_id=1, replica_groups=mesh['cells'=8,'seq'=4] {'seq'}, dimensions={0} | all-to-all | bytes 4300800 | tf_op jit(solution)/shard_map/all_to_all | solution.py:253
  640.1 12.7 reshape.830
  652.8 11.0 copy.105
  665.6 8.4 convolution_bitcast_fusion
  674.0 11.8 copy.108
  685.9 5.5 copy.112
  691.4 8.5 fusion.64
  700.0 104.3 %all_to_all.134 = f32[1120,4,280]{0,2,1:T(8,128)} all-to-all(f32[1120,4,280]{0,2,1:T(8,128)S(1)} %fusion.64), channel_id=1, replica_groups=mesh['cells'=8,'seq'=4] {'seq'}, dimensions={1} | all-to-all | bytes 10035200 | tf_op jit(solution)/shard_map/all_to_all | solution.py:235
  804.3 6.8 copy.129
  811.2 5.4 copy.110
  816.6 6.7 fusion.66
  823.3 77.0 %all_to_all.135 = f32[1120,4,280]{0,2,1:T(8,128)} all-to-all(f32[1120,4,280]{0,2,1:T(8,128)S(1)} %fusion.66), channel_id=1, replica_groups=mesh['cells'=8,'seq'=4] {'seq'}, dimensions={1} | all-to-all | bytes 10035200 | tf_op jit(solution)/shard_map/all_to_all | solution.py:234
  900.2 6.7 copy.128
  913.0 7.6 fusion.107
  923.4 6.4 all-reduce.2
  929.9 22.3 %psum.52 = f32[2,280]{1,0:T(2,128)} all-reduce(f32[2,280]{1,0:T(2,128)S(1)} %constant_dynamic-slice_fusion), channel_id=1, replica_groups=mesh['cells'=8,'seq'=4] {'cells'}, use_global_device_ids=true, to_apply=%region_26.27 | all-reduce | flops 560 | bytes 4480 | tf_op jit(solution)/shard_map/psum | solution.py:265
  952.2 41.3 %all-reduce.4 = (f32[2,1120]{1,0:T(2,128)}, f32[2,1120]{1,0:T(2,128)}, f32[2,1120]{1,0:T(2,128)}, f32[4480]{0:T(1024)}) all-reduce(f32[2,1120]{1,0:T(2,128)S(1)} %pad_maximum_fusion.2, f32[2,1120]{1,0:T(2,128)S(1)} %pad_maximum_fusion.3, f32[2,1120]{1,0:T(2,128)S(1)} %pad_maximum_fusion.5, ...), channel_id=1, replica_groups=mesh['cells'=8,'seq'=4] {'cells','seq'}, use_global_device_ids=true, to_apply=%region_18.19 | all-reduce | flops 11200 | bytes 89600 | tf_op jit(solution)/shard_map/psum | solution.py:268
  996.4 127.5 %reduce-scatter.20.cloned.1.call-done = f32[560,280]{1,0:T(8,128)} async-done(((f32[4480,280]{1,0:T(8,128)}), f32[560,280]{1,0:T(8,128)}) %reduce-scatter.20.cloned.1.call-update) | async-done | bytes 627216
  1126.2 183.0 %all-reduce.8.cloned.1.call-done = (f32[3,1120,280]{1,2,0:T(8,128)}, f32[280,1120]{1,0:T(8,128)}) async-done(((f32[3,1120,280]{1,2,0:T(8,128)}, f32[280,1120]{1,0:T(8,128)}), (f32[3,1120,280]{1,2,0:T(8,128)}, f32[280,1120]{1,0:T(8,128)})) %all-reduce.8.cloned.1.call-update) | async-done | bytes 5017616 | tf_op jit(solution)/shard_map/psum | solution.py:265
  1309.2 4.3 copy.141
  (181 shorter events, 65.9 us)
Async XLA Ops:
  7.2 59.7 %all-gather.10.cloned.1.call-start = ((), (), s32[]{:S(2)}) async-start(), calls=%async_computation.14 | async-start | bytes 9676800 | tf_op jit(solution)/shard_map/all_gather | solution.py:175
  7.9 183.1 %all-gather.12.cloned.1.call-start = ((), (), s32[]{:S(2)}) async-start(), calls=%async_computation.15 | async-start | bytes 3225600 | tf_op jit(solution)/shard_map/all_gather | solution.py:176
  8.7 188.3 %all-gather.18.cloned.1.call-start = ((), (), s32[]{:S(2)}) async-start(), calls=%async_computation.21 | async-start | bytes 3225600 | tf_op jit(solution)/shard_map/all_gather | solution.py:160
  17.5 56.8 %copy-start.21 = (f32[1120]{0:T(1024)}, f32[1120]{0:T(1024)S(1)}, u32[]{:S(2)}) copy-start(f32[1120]{0:T(1024)S(1)} %get-tuple-element.85) | copy-start | bytes 13444
  17.6 56.8 %copy-start.27 = (f32[1120]{0:T(1024)}, f32[1120]{0:T(1024)S(1)}, u32[]{:S(2)}) copy-start(f32[1120]{0:T(1024)S(1)} %get-tuple-element.87) | copy-start | bytes 13444
  19.0 55.4 %copy-start.23 = (f32[320]{0:T(512)}, f32[320]{0:T(512)S(1)}, u32[]{:S(2)}) copy-start(f32[320]{0:T(512)S(1)} %broadcast_multiply_fusion.1) | copy-start | bytes 3844
  20.6 0.6 copy-start.29
  21.2 53.2 %copy-start.25 = (f32[320]{0:T(512)}, f32[320]{0:T(512)S(1)}, u32[]{:S(2)}) copy-start(f32[320]{0:T(512)S(1)} %fusion.148) | copy-start | bytes 3844
  76.8 43.2 %all-to-all-start = ((bf16[1,320,4,5,3,56]{1,5,3,4,0,2:T(8,128)(2,1)}), bf16[1,320,4,5,3,56]{1,5,3,4,0,2:T(8,128)(2,1)S(1)}, u32[]{:S(2)}, u32[]{:S(2)}) async-start(bf16[1,320,4,5,3,56]{1,5,3,4,0,2:T(8,128)(2,1)} %copy.87), calls=%async_computation | async-start | bytes 5160960 | tf_op jit(solution)/shard_map/all_to_all | solution.py:186
  80.4 140.4 %all-gather.20.cloned.1.call-start = ((), (), s32[]{:S(2)}) async-start(), calls=%async_computation.22 | async-start | bytes 3225600 | tf_op jit(solution)/shard_map/all_gather | solution.py:161
  82.6 57.8 %copy-start.13 = (pred[640,640]{0,1:T(8,128)(4,1)}, pred[640,640]{0,1:T(8,128)(4,1)S(1)}, u32[]{:S(2)}) copy-start(pred[640,640]{0,1:T(8,128)(4,1)S(1)} %fusion.101) | copy-start | bytes 1228804
  126.9 26.0 %copy-start.1 = (bf16[1,1280,5,3,56]{1,4,2,3,0:T(8,128)(2,1)}, bf16[1,1280,5,3,56]{1,4,2,3,0:T(8,128)(2,1)S(1)}, u32[]{:S(2)}) copy-start(bf16[1,1280,5,3,56]{1,4,2,3,0:T(8,128)(2,1)S(1)} %squeeze.15) | copy-start | bytes 6451204
  127.1 9.2 copy-start.15
  127.1 9.1 copy-start.18
  127.1 13.4 %copy-start.16 = (bf16[1,1280,5,56]{1,3,2,0:T(8,128)(2,1)}, bf16[1,1280,5,56]{1,3,2,0:T(8,128)(2,1)S(1)}, u32[]{:S(2)}) copy-start(bf16[1,1280,5,56]{1,3,2,0:T(8,128)(2,1)S(1)} %get-tuple-element.100) | copy-start | bytes 2150404
  137.8 5.4 copy-start.7
  162.1 11.0 copy-start.32
  165.0 26.0 %copy-start = (bf16[1,320,1120]{2,1,0:T(8,128)(2,1)S(1)}, bf16[1,320,1120]{2,1,0:T(8,128)(2,1)}, u32[]{:S(2)}) copy-start(bf16[1,320,1120]{2,1,0:T(8,128)(2,1)} %param.25) | copy-start | bytes 2150404
  168.8 15.2 %all-to-all-start.1 = ((bf16[4,2,44800]{2,1,0:T(2,128)(2,1)}), bf16[4,2,44800]{2,1,0:T(2,128)(2,1)}, u32[]{:S(2)}, u32[]{:S(2)}) async-start(bf16[4,2,44800]{2,1,0:T(2,128)(2,1)} %reshape.827), calls=%async_computation.1 | async-start | bytes 1433600 | tf_op jit(solution)/shard_map/all_to_all | solution.py:189
  173.0 92.5 %all-gather.14.cloned.1.call-start = ((), (), s32[]{:S(2)}) async-start(), calls=%async_computation.16 | async-start | bytes 3686400 | tf_op jit(solution)/shard_map/all_gather | solution.py:199
  196.3 111.3 %all-gather.16.cloned.1.call-start = ((), (), s32[]{:S(2)}) async-start(), calls=%async_computation.18 | async-start | bytes 3686400 | tf_op jit(solution)/shard_map/all_gather | solution.py:200
  210.2 49.9 %all-to-all-start.2 = ((bf16[4,1120,280]{1,2,0:T(8,128)(2,1)}), bf16[4,1120,280]{1,2,0:T(8,128)(2,1)}, u32[]{:S(2)}, u32[]{:S(2)}) async-start(bf16[4,1120,280]{1,2,0:T(8,128)(2,1)} %copy.93), calls=%async_computation.2 | async-start | bytes 5160960 | tf_op jit(solution)/shard_map/all_to_all | solution.py:164
  260.1 51.3 %all-to-all-start.3 = ((bf16[4,1120,280]{1,2,0:T(8,128)(2,1)}), bf16[4,1120,280]{1,2,0:T(8,128)(2,1)}, u32[]{:S(2)}, u32[]{:S(2)}) async-start(bf16[4,1120,280]{1,2,0:T(8,128)(2,1)} %copy.95), calls=%async_computation.3 | async-start | bytes 5160960 | tf_op jit(solution)/shard_map/all_to_all | solution.py:165
  264.7 124.9 %reduce-scatter.16.cloned.1.call-start = ((), (), s32[]{:S(2)}) async-start(), calls=%async_computation.19 | async-start | bytes 7372800 | tf_op jit(solution)/shard_map/reduce_scatter | solution.py:232
  324.2 1.5 copy-start.34
  333.9 95.8 %reduce-scatter.14.cloned.1.call-start = ((), (), s32[]{:S(2)}) async-start(), calls=%async_computation.17 | async-start | bytes 3686400 | tf_op jit(solution)/shard_map/reduce_scatter | solution.py:213
  344.4 562.7 %reduce-scatter.24.cloned.1.call-start = ((), (), s32[]{:S(2)}) async-start(), calls=%async_computation.25 | async-start | bytes 6451200
  391.5 42.6 %copy-start.6 = (bf16[1,4,320,5,56]{2,4,3,1,0:T(8,128)(2,1)S(1)}, bf16[1,4,320,5,56]{2,4,3,1,0:T(8,128)(2,1)}, u32[]{:S(2)}) copy-start(bf16[1,4,320,5,56]{2,4,3,1,0:T(8,128)(2,1)} %copy.91) | copy-start | bytes 2150404
  429.6 4.2 copy-start.9
  432.7 1.1 copy-start.4
  442.3 15.9 %all-to-all-start.4 = ((bf16[1,320,20,56]{1,3,0,2:T(8,128)(2,1)}), bf16[1,320,20,56]{1,3,0,2:T(8,128)(2,1)S(1)}, u32[]{:S(2)}, u32[]{:S(2)}) async-start(bf16[1,320,20,56]{1,3,0,2:T(8,128)(2,1)} %bitcast.48), calls=%async_computation.6 | async-start | bytes 1720320 | tf_op jit(solution)/shard_map/all_to_all | solution.py:251
  445.8 461.2 %reduce-scatter.18.cloned.1.call-start = ((), (), s32[]{:S(2)}) async-start(), calls=%async_computation.20 | async-start | bytes 19353600 | tf_op jit(solution)/shard_map/reduce_scatter | solution.py:261
  458.6 6.4 copy-start.14
  459.2 5.7 copy-start.11
  459.3 5.7 copy-start.19
  482.3 17.6 %copy-start.2 = (bf16[1,1280,5,3,56]{1,4,2,3,0:T(8,128)(2,1)S(1)}, bf16[1,1280,5,3,56]{1,4,2,3,0:T(8,128)(2,1)}, u32[]{:S(2)}) copy-start(bf16[1,1280,5,3,56]{1,4,2,3,0:T(8,128)(2,1)} %copy-done.1) | copy-start | bytes 6451204
  578.8 6.0 copy-start.8
  578.8 6.0 copy-start.12
  584.8 8.4 copy-start.20
  652.8 12.8 copy-start.22
  652.8 12.8 copy-start.24
  652.8 12.8 copy-start.26
  652.8 12.8 copy-start.28
  664.1 1.4 copy-start.3
  685.8 308.2 %reduce-scatter.22.cloned.1.call-start = ((), (), s32[]{:S(2)}) async-start(), calls=%async_computation.24 | async-start | bytes 7741440
  811.2 312.7 %reduce-scatter.20.cloned.1.call-start = ((), (), s32[]{:S(2)}) async-start(), calls=%async_computation.23 | async-start | bytes 7741440
  906.9 0.8 copy-start.33
  906.9 2.0 copy-start.31
  907.0 402.2 %all-reduce.8.cloned.1.call-start = ((), (), s32[]{:S(2)}) async-start(), calls=%async_computation.26 | async-start | bytes 10321920 | tf_op jit(solution)/shard_map/psum | solution.py:265
  913.0 7.7 copy-start.30
  913.0 8.5 copy-start.5
  913.0 8.5 copy-start.10
  1309.2 4.4 copy-start.17
Sparse Core Ops, SparseCore 0:
  9.6 57.3 all-gather.9
  68.5 34.0 all-gather.11
  104.8 57.7 all-gather.17
  164.7 56.1 all-gather.19
  222.8 40.0 all-gather.13
  264.4 43.2 all-gather.15
  334.0 55.5 reduce-scatter.15
  392.9 36.7 reduce-scatter.13
  438.1 50.8 reduce-scatter.23
  686.0 175.8 reduce-scatter.17
  865.9 128.0 reduce-scatter.21
  998.0 125.7 reduce-scatter.19
  1128.0 181.1 all-reduce.7
where the time goes:
time: 1330 us; the launch traced here: 1320 us
  waiting for transfers between devices  571 us (43%)
  blocking collectives  287 us (22%)
  matrix products  245 us (18%)
  local copies, waits for them, and re-layouts  147 us (11%)
  other arithmetic  33.3 us (3%)
  starting transfers between devices  21.5 us (2%)
  between operations  16.9 us (1%)
    psum x1, waiting for transfers between devices, body(): lax.psum((grad_qkv_own, grad_bias_own, grad_out_own), 'cells')  183 us
    unnamed x16, waiting for transfers between devices  132 us
    all_to_all x1, blocking collectives, body(): lax.all_to_all(grad_down_unit, 'seq', split_axis=1, concat_axis=0, tiled=...  104 us
    all_to_all x1, blocking collectives, body(): lax.all_to_all(grad_up_unit, 'seq', split_axis=1, concat_axis=0, tiled=True)  77 us
    unnamed x83, local copies, waits for them, and re-layouts  60.8 us
    dot_general x2, matrix products, attend_back(): jnp.einsum('chqk,cqhe->ckhe', grad_scores, queries[:, start_row:end_row],...  52.7 us
    dot_general x2, matrix products, attend_back(): jnp.einsum('chqk,ckhe->cqhe', grad_scores, keys_all[:, :end_row], preferr...  50.9 us
    all_gather x1, waiting for transfers between devices, body(): lax.all_gather(w_qkv, 'seq', axis=2, tiled=True)  45.7 us
  transfers between devices with their start and end apart: 18, of which 13 were waited for; matrix products, arithmetic and copies ran while one was open for 28% of the time, Pallas kernels for 0%

commit v1 on v0

--- a/solution.py
+++ b/solution.py
@@ -9,6 +9,36 @@
 QBLOCK = 640
 epsilon = 1e-05
 masked_score = -1e30
+
+
+def knots_search(block_in, dim_k):
+    n_now, everything, s_next = (
+        jax.lax.axis_size("seq"),
+        jax.lax.axis_index("seq"),
+        block_in.shape[dim_k],
+    )
+    by_place = tuple(
+        (dev_j * n_now if b == dim_k else dev_j for b, dev_j in enumerate(block_in.shape))
+    )
+    z1 = lax.dynamic_update_slice_in_dim(
+        jnp.zeros(by_place, block_in.dtype), block_in, everything * s_next, axis=dim_k
+    )
+    found_now = k_now = block_in
+    for at in [*range(1, n_now // 2 + 1)]:
+        found_now = jax.lax.ppermute(
+            found_now, "seq", tuple(((b, (b + 1) % n_now) for b in range(n_now)))
+        )
+        z1 = lax.dynamic_update_slice_in_dim(
+            z1, found_now, (everything - at) % n_now * s_next, axis=dim_k
+        )
+        if 2 * at < n_now:
+            k_now = jax.lax.ppermute(
+                k_now, "seq", tuple(((b, (b - 1) % n_now) for b in range(n_now)))
+            )
+            z1 = lax.dynamic_update_slice_in_dim(
+                z1, k_now, (everything + at) % n_now * s_next, axis=dim_k
+            )
+    return z1
 
 
 def layer_norm(rows, gain, shift):
@@ -197,7 +227,7 @@
     normed2 = normed2_f.astype(jnp.bfloat16)
     normed2_all, grad_all = (
         lax.all_gather(normed2, "seq", axis=1, tiled=True),
-        lax.all_gather(out_grad, "seq", axis=1, tiled=True),
+        knots_search(out_grad, 1),
     )
     units = up_unit.shape[0]
     first_unit = lax.axis_index("seq") * units

time: 1330 us -> 1370 us (1.030)
  local copies, waits for them, and re-layouts: 147 us -> 189 us
    dynamic_update_slice x0 -> x4, local copies, waits for them, and re-layouts: none -> 37.5 us  [the longest x2 18.4 us: knots_search(): lax.dynamic_update_slice_in_dim(z1, found_now, (everything - at) % n_now...]
    all_gather x1 -> x0, waiting for transfers between devices: 33.1 us -> none  [body(): lax.all_gather(out_grad, 'seq', axis=1, tiled=True)]
    ppermute x0 -> x3, waiting for transfers between devices: none -> 29.8 us  [the longest x1 26 us: knots_search(): jax.lax.ppermute(k_now, 'seq', tuple(((b, (b - 1) % n_now) for b in range...]
    unnamed x16 -> x15, waiting for transfers between devices: 132 us -> 138 us
    unnamed x83 -> x85, local copies, waits for them, and re-layouts: 60.8 us -> 60.5 us
  transfers between devices with their start and end apart: 18 -> 20, of which waited for: 13 -> 13; matrix products, arithmetic and copies ran while one was open for 28% -> 30% of each run, Pallas kernels for 0% -> 0%
where the time goes in v1:
time: 1370 us; the launch traced here: 1360 us
  waiting for transfers between devices  571 us (42%)
  blocking collectives  286 us (21%)
  matrix products  244 us (18%)
  local copies, waits for them, and re-layouts  189 us (14%)
  other arithmetic  33.3 us (2%)
  starting transfers between devices  24 us (2%)
  between operations  17.2 us (1%)
    psum x1, waiting for transfers between devices, body(): lax.psum((grad_qkv_own, grad_bias_own, grad_out_own), 'cells')  183 us
    unnamed x15, waiting for transfers between devices  138 us
    all_to_all x1, blocking collectives, body(): lax.all_to_all(grad_down_unit, 'seq', split_axis=1, concat_axis=0, tiled=...  98.1 us
    all_to_all x1, blocking collectives, body(): lax.all_to_all(grad_up_unit, 'seq', split_axis=1, concat_axis=0, tiled=True)  83.3 us
    unnamed x85, local copies, waits for them, and re-layouts  60.5 us
    dot_general x2, matrix products, attend_back(): jnp.einsum('chqk,cqhe->ckhe', grad_scores, queries[:, start_row:end_row],...  52.7 us
    dot_general x2, matrix products, attend_back(): jnp.einsum('chqk,ckhe->cqhe', grad_scores, keys_all[:, :end_row], preferr...  50.9 us
    reduce_scatter x1, waiting for transfers between devices, body(): lax.psum_scatter(normed2_terms, 'seq', scatter_dimension=1, tiled=True)  46.2 us
  transfers between devices with their start and end apart: 20, of which 13 were waited for; matrix products, arithmetic and copies ran while one was open for 30% of the time, Pallas kernels for 0%

profile of v1, /device:TPU:0, one launch (start us, length us, event | category | flops | bytes accessed | tf_op | source)
XLA Modules:
  0.0 1364.1 jit_solution(8395270514615228451)
XLA Ops:
  9.4 6.3 all-gather
  21.3 45.7 %all-gather.9.cloned.1.call-done = bf16[3,1120,1120]{1,2,0:T(8,128)(2,1)} async-done(((bf16[3,1120,280]{1,2,0:T(8,128)(2,1)}), bf16[3,1120,1120]{1,2,0:T(8,128)(2,1)}) %all-gather.9.cloned.1.call-update) | async-done | bytes 7526416 | tf_op jit(solution)/shard_map/all_gather | solution.py:205
  66.9 7.4 fusion.131
  84.5 35.4 %all-to-all-done = bf16[1,320,4,5,3,56]{1,5,3,4,0,2:T(8,128)(2,1)S(1)} async-done(((bf16[1,320,4,5,3,56]{1,5,3,4,0,2:T(8,128)(2,1)}), bf16[1,320,4,5,3,56]{1,5,3,4,0,2:T(8,128)(2,1)S(1)}, u32[]{:S(2)}, u32[]{:S(2)}) %all-to-all-start) | async-done | bytes 2150432 | tf_op jit(solution)/shard_map/all_to_all | solution.py:216
  122.4 4.5 squeeze.15
  127.1 9.1 fusion.178
  143.2 9.6 fusion.6
  152.9 9.1 fusion.118
  165.0 3.8 reshape.844
  168.8 4.2 all-to-all-start.1
  173.1 10.9 all-to-all-done.1
  184.0 4.4 reshape.845
  191.0 3.7 fusion.179
  196.3 3.8 copy.104
  200.1 6.0 all_to_all.104
  209.7 4.6 all-to-all-start.2
  214.7 6.1 all-gather.17.cloned.1.call-done
  224.6 6.1 all_to_all.108
  234.2 25.4 %all-to-all-done.2 = bf16[4,1120,280]{1,2,0:T(8,128)(2,1)} async-done(((bf16[4,1120,280]{1,2,0:T(8,128)(2,1)}), bf16[4,1120,280]{1,2,0:T(8,128)(2,1)}, u32[]{:S(2)}, u32[]{:S(2)}) %all-to-all-start.2) | async-done | bytes 2508832 | tf_op jit(solution)/shard_map/all_to_all | solution.py:194
  259.6 4.6 all-to-all-start.3
  265.9 3.8 collective-permute-done
  273.0 9.2 dynamic_update_slice.19
  283.0 26.0 %collective-permute-done.1 = bf16[1,320,1120]{2,1,0:T(8,128)(2,1)} collective-permute-done((bf16[1,320,1120]{2,1,0:T(8,128)(2,1)S(1)}, bf16[1,320,1120]{2,1,0:T(8,128)(2,1)}, u32[]{:S(2)}, u32[]{:S(2)}) %collective-permute-start.1) | collective-permute-done | bytes 716832 | tf_op jit(solution)/shard_map/ppermute | solution.py:35
  313.4 9.6 dynamic_update_slice.20
  323.1 9.9 dynamic_update_slice.21
  335.3 8.7 dynamic_update_slice.22
  344.1 9.1 convolution_add_fusion
  353.1 12.0 convert_reduce_fusion
  366.7 8.5 convolution_bitcast_fusion.1
  375.3 10.8 fusion.36
  386.1 46.2 %reduce-scatter.16.cloned.1.call-done = f32[1,320,1120]{2,1,0:T(8,128)} async-done(((f32[1,1280,1120]{2,1,0:T(8,128)}), f32[1,320,1120]{2,1,0:T(8,128)}) %reduce-scatter.16.cloned.1.call-update) | async-done | bytes 1433616 | tf_op jit(solution)/shard_map/reduce_scatter | solution.py:262
  434.3 38.1 %reduce-scatter.14.cloned.1.call-done = bf16[1,320,1120]{2,1,0:T(8,128)(2,1)} async-done(((bf16[1,1280,1120]{2,1,0:T(8,128)(2,1)}), bf16[1,320,1120]{2,1,0:T(8,128)(2,1)}) %reduce-scatter.14.cloned.1.call-update) | async-done | bytes 716816 | tf_op jit(solution)/shard_map/reduce_scatter | solution.py:243
  476.9 3.9 fusion.128
  488.9 12.2 all-to-all-done.4
  502.0 5.7 fusion.142
  507.8 17.3 %fusion.119 = bf16[1,640,5,56]{1,3,2,0:T(8,128)(2,1)} fusion(f32[5,640,640]{1,2,0:T(8,128)} %fusion.142, bf16[1,1280,5,56]{1,3,2,0:T(8,128)(2,1)S(1)} %copy-done.20, f32[5,640,640]{1,2,0:T(8,128)} %copy-done.7, f32[5,640]{1,0:T(8,128)S(1)} %log_add_fusion.1, pred[640,640]{0,1:T(8,128)(4,1)S(1)} %copy-done.15), kind=kOutput, calls=%fused_computation.122 | convolution fusion | flops 256183040 | bytes 34344960 | tf_op jit(solution)/shard_map/chqk,ckhe->cqhe/dot_general | solution.py:128
  525.1 17.6 %fusion.107 = f32[1,640,5,56]{1,3,2,0:T(8,128)} fusion(f32[5,640,640]{1,2,0:T(8,128)} %fusion.142, bf16[1,1280,5,56]{1,3,2,0:T(8,128)(2,1)} %copy-done.16, f32[5,640,640]{1,2,0:T(8,128)} %copy-done.7, f32[5,640]{1,0:T(8,128)S(1)} %log_add_fusion.1, pred[640,640]{0,1:T(8,128)(4,1)S(1)} %copy-done.15), kind=kOutput, calls=%fused_computation.116 | convolution fusion | flops 256003840 | bytes 34703360 | tf_op jit(solution)/shard_map/chqk,cqhe->ckhe/dot_general | solution.py:136
  542.7 9.0 fusion.135
  551.7 35.0 %fusion.87 = bf16[1,1280,5,1,56]{1,4,2,3,0:T(8,128)(2,1)} fusion(f32[5,640,1280]{2,1,0:T(8,128)} %fusion.135, f32[5,640,1280]{2,1,0:T(8,128)} %get-tuple-element.109, f32[5,640]{1,0:T(8,128)S(1)} %log_add_fusion, pred[640,1280]{1,0:T(8,128)(4,1)} %fusion.57, f32[1,640,5,56]{1,3,2,0:T(8,128)} %fusion.107, bf16[1,1280,5,56]{1,3,2,0:T(8,128)(2,1)} %copy-done.16), kind=kOutput, calls=%fused_computation.82 | convolution fusion | flops 496337280 | bytes 69007360 | tf_op jit(solution)/shard_map/chqk,cqhe->ckhe/dot_general | solution.py:136
  586.8 33.6 %fusion.123 = bf16[1,640,5,56]{1,3,2,0:T(8,128)(2,1)} fusion(f32[5,640,1280]{2,1,0:T(8,128)} %fusion.135, f32[5,640,1280]{2,1,0:T(8,128)} %get-tuple-element.109, f32[5,640]{1,0:T(8,128)S(1)} %log_add_fusion, pred[640,1280]{1,0:T(8,128)(4,1)} %fusion.57, bf16[1,1280,5,3,56]{1,4,2,3,0:T(8,128)(2,1)S(1)} %copy-done.2), kind=kOutput, calls=%fused_computation.124 | convolution fusion | flops 495799680 | bytes 68290560 | tf_op jit(solution)/shard_map/chqk,ckhe->cqhe/dot_general | solution.py:128
  621.6 6.0 fusion.104
  627.6 8.4 fusion.84
  636.2 6.3 copy.121
  642.5 10.7 reshape.846
  653.2 29.5 %all_to_all.133 = bf16[4,2,134400]{2,1,0:T(2,128)(2,1)} all-to-all(bf16[4,2,134400]{2,1,0:T(2,128)(2,1)S(1)} %reshape.846), channel_id=1, replica_groups=mesh['cells'=8,'seq'=4] {'seq'}, dimensions={0} | all-to-all | bytes 4300800 | tf_op jit(solution)/shard_map/all_to_all | solution.py:283
  682.8 12.7 reshape.847
  695.5 11.0 copy.122
  708.3 8.4 convolution_bitcast_fusion
  716.7 11.8 copy.125
  728.8 7.5 fusion.60
  736.3 98.1 %all_to_all.134 = f32[1120,4,280]{0,2,1:T(8,128)} all-to-all(f32[1120,4,280]{0,2,1:T(8,128)S(1)} %fusion.60), channel_id=1, replica_groups=mesh['cells'=8,'seq'=4] {'seq'}, dimensions={1} | all-to-all | bytes 10035200 | tf_op jit(solution)/shard_map/all_to_all | solution.py:265
  834.5 6.6 copy.146
  841.1 5.5 copy.127
  846.6 6.6 fusion.62
  853.3 83.3 %all_to_all.135 = f32[1120,4,280]{0,2,1:T(8,128)} all-to-all(f32[1120,4,280]{0,2,1:T(8,128)S(1)} %fusion.62), channel_id=1, replica_groups=mesh['cells'=8,'seq'=4] {'seq'}, dimensions={1} | all-to-all | bytes 10035200 | tf_op jit(solution)/shard_map/all_to_all | solution.py:264
  936.6 6.6 copy.145
  949.0 7.6 fusion.103
  959.4 6.4 all-reduce.2
  965.8 22.2 %psum.52 = f32[2,280]{1,0:T(2,128)} all-reduce(f32[2,280]{1,0:T(2,128)S(1)} %constant_dynamic-slice_fusion), channel_id=1, replica_groups=mesh['cells'=8,'seq'=4] {'cells'}, use_global_device_ids=true, to_apply=%region_26.27 | all-reduce | flops 560 | bytes 4480 | tf_op jit(solution)/shard_map/psum | solution.py:295
  988.0 40.5 %all-reduce.4 = (f32[2,1120]{1,0:T(2,128)}, f32[2,1120]{1,0:T(2,128)}, f32[2,1120]{1,0:T(2,128)}, f32[4480]{0:T(1024)}) all-reduce(f32[2,1120]{1,0:T(2,128)S(1)} %pad_maximum_fusion.2, f32[2,1120]{1,0:T(2,128)S(1)} %pad_maximum_fusion.3, f32[2,1120]{1,0:T(2,128)S(1)} %pad_maximum_fusion.5, ...), channel_id=1, replica_groups=mesh['cells'=8,'seq'=4] {'cells','seq'}, use_global_device_ids=true, to_apply=%region_18.19 | all-reduce | flops 11200 | bytes 89600 | tf_op jit(solution)/shard_map/psum | solution.py:298
  1028.5 8.2 reduce-scatter.22.cloned.1.call-done
  1039.0 127.4 %reduce-scatter.20.cloned.1.call-done = f32[560,280]{1,0:T(8,128)} async-done(((f32[4480,280]{1,0:T(8,128)}), f32[560,280]{1,0:T(8,128)}) %reduce-scatter.20.cloned.1.call-update) | async-done | bytes 627216
  1168.8 182.9 %all-reduce.8.cloned.1.call-done = (f32[3,1120,280]{1,2,0:T(8,128)}, f32[280,1120]{1,0:T(8,128)}) async-done(((f32[3,1120,280]{1,2,0:T(8,128)}, f32[280,1120]{1,0:T(8,128)}), (f32[3,1120,280]{1,2,0:T(8,128)}, f32[280,1120]{1,0:T(8,128)})) %all-reduce.8.cloned.1.call-update) | async-done | bytes 5017616 | tf_op jit(solution)/shard_map/psum | solution.py:295
  1351.6 4.3 copy.162
  (194 shorter events, 91.4 us)
Async XLA Ops:
  7.2 59.7 %all-gather.9.cloned.1.call-start = ((), (), s32[]{:S(2)}) async-start(), calls=%async_computation.14 | async-start | bytes 9676800 | tf_op jit(solution)/shard_map/all_gather | solution.py:205
  7.9 183.1 %all-gather.11.cloned.1.call-start = ((), (), s32[]{:S(2)}) async-start(), calls=%async_computation.15 | async-start | bytes 3225600 | tf_op jit(solution)/shard_map/all_gather | solution.py:206
  8.7 187.6 %all-gather.15.cloned.1.call-start = ((), (), s32[]{:S(2)}) async-start(), calls=%async_computation.20 | async-start | bytes 3225600 | tf_op jit(solution)/shard_map/all_gather | solution.py:190
  17.5 56.8 %copy-start.22 = (f32[1120]{0:T(1024)}, f32[1120]{0:T(1024)S(1)}, u32[]{:S(2)}) copy-start(f32[1120]{0:T(1024)S(1)} %get-tuple-element.85) | copy-start | bytes 13444
  17.6 56.8 %copy-start.28 = (f32[1120]{0:T(1024)}, f32[1120]{0:T(1024)S(1)}, u32[]{:S(2)}) copy-start(f32[1120]{0:T(1024)S(1)} %get-tuple-element.87) | copy-start | bytes 13444
  19.0 55.4 %copy-start.24 = (f32[320]{0:T(512)}, f32[320]{0:T(512)S(1)}, u32[]{:S(2)}) copy-start(f32[320]{0:T(512)S(1)} %broadcast_multiply_fusion.1) | copy-start | bytes 3844
  20.6 0.6 copy-start.30
  21.2 53.2 %copy-start.26 = (f32[320]{0:T(512)}, f32[320]{0:T(512)S(1)}, u32[]{:S(2)}) copy-start(f32[320]{0:T(512)S(1)} %fusion.144) | copy-start | bytes 3844
  76.8 43.2 %all-to-all-start = ((bf16[1,320,4,5,3,56]{1,5,3,4,0,2:T(8,128)(2,1)}), bf16[1,320,4,5,3,56]{1,5,3,4,0,2:T(8,128)(2,1)S(1)}, u32[]{:S(2)}, u32[]{:S(2)}) async-start(bf16[1,320,4,5,3,56]{1,5,3,4,0,2:T(8,128)(2,1)} %copy.99), calls=%async_computation | async-start | bytes 5160960 | tf_op jit(solution)/shard_map/all_to_all | solution.py:216
  80.4 140.4 %all-gather.17.cloned.1.call-start = ((), (), s32[]{:S(2)}) async-start(), calls=%async_computation.21 | async-start | bytes 3225600 | tf_op jit(solution)/shard_map/all_gather | solution.py:191
  82.6 57.8 %copy-start.14 = (pred[640,640]{0,1:T(8,128)(4,1)}, pred[640,640]{0,1:T(8,128)(4,1)S(1)}, u32[]{:S(2)}) copy-start(pred[640,640]{0,1:T(8,128)(4,1)S(1)} %fusion.97) | copy-start | bytes 1228804
  126.9 26.0 %copy-start.1 = (bf16[1,1280,5,3,56]{1,4,2,3,0:T(8,128)(2,1)}, bf16[1,1280,5,3,56]{1,4,2,3,0:T(8,128)(2,1)S(1)}, u32[]{:S(2)}) copy-start(bf16[1,1280,5,3,56]{1,4,2,3,0:T(8,128)(2,1)S(1)} %squeeze.15) | copy-start | bytes 6451204
  127.1 9.2 copy-start.16
  127.1 9.1 copy-start.19
  127.1 13.4 copy-start.17
  137.8 5.4 copy-start.7
  162.0 11.0 copy-start.33
  165.0 26.0 %copy-start = (bf16[1,320,1120]{2,1,0:T(8,128)(2,1)S(1)}, bf16[1,320,1120]{2,1,0:T(8,128)(2,1)}, u32[]{:S(2)}) copy-start(bf16[1,320,1120]{2,1,0:T(8,128)(2,1)} %param.25) | copy-start | bytes 2150404
  168.8 15.2 %all-to-all-start.1 = ((bf16[4,2,44800]{2,1,0:T(2,128)(2,1)}), bf16[4,2,44800]{2,1,0:T(2,128)(2,1)}, u32[]{:S(2)}, u32[]{:S(2)}) async-start(bf16[4,2,44800]{2,1,0:T(2,128)(2,1)} %reshape.844), calls=%async_computation.1 | async-start | bytes 1433600 | tf_op jit(solution)/shard_map/all_to_all | solution.py:219
  173.0 171.1 %all-gather.13.cloned.1.call-start = ((), (), s32[]{:S(2)}) async-start(), calls=%async_computation.16 | async-start | bytes 3686400 | tf_op jit(solution)/shard_map/all_gather | solution.py:229
  206.1 8.2 copy-start.9
  209.7 49.9 %all-to-all-start.2 = ((bf16[4,1120,280]{1,2,0:T(8,128)(2,1)}), bf16[4,1120,280]{1,2,0:T(8,128)(2,1)}, u32[]{:S(2)}, u32[]{:S(2)}) async-start(bf16[4,1120,280]{1,2,0:T(8,128)(2,1)} %copy.105), calls=%async_computation.2 | async-start | bytes 5160960 | tf_op jit(solution)/shard_map/all_to_all | solution.py:194
  214.3 55.5 %collective-permute-start = (bf16[1,320,1120]{2,1,0:T(8,128)(2,1)S(1)}, bf16[1,320,1120]{2,1,0:T(8,128)(2,1)}, u32[]{:S(2)}, u32[]{:S(2)}) collective-permute-start(bf16[1,320,1120]{2,1,0:T(8,128)(2,1)S(1)} %copy-done.9), channel_id=1, source_target_pairs={{0,1},{1,2},{2,3},{3,0},{4,5},{5,6},{6,7},{7,4},{8,9},{9,10},{10,1... | collective-permute-start | bytes 2150408 | tf_op jit(solution)/shard_map/ppermute | solution.py:28
  259.6 93.6 %all-to-all-start.3 = ((bf16[4,1120,280]{1,2,0:T(8,128)(2,1)}), bf16[4,1120,280]{1,2,0:T(8,128)(2,1)}, u32[]{:S(2)}, u32[]{:S(2)}) async-start(bf16[4,1120,280]{1,2,0:T(8,128)(2,1)} %copy.107), calls=%async_computation.3 | async-start | bytes 5160960 | tf_op jit(solution)/shard_map/all_to_all | solution.py:195
  264.2 168.2 %reduce-scatter.16.cloned.1.call-start = ((), (), s32[]{:S(2)}) async-start(), calls=%async_computation.18 | async-start | bytes 7372800 | tf_op jit(solution)/shard_map/reduce_scatter | solution.py:262
  264.2 44.7 %collective-permute-start.1 = (bf16[1,320,1120]{2,1,0:T(8,128)(2,1)S(1)}, bf16[1,320,1120]{2,1,0:T(8,128)(2,1)}, u32[]{:S(2)}, u32[]{:S(2)}) collective-permute-start(bf16[1,320,1120]{2,1,0:T(8,128)(2,1)S(1)} %copy-done.9), channel_id=1, source_target_pairs={{0,3},{1,0},{2,1},{3,2},{4,7},{5,4},{6,5},{7,6},{8,11},{9,8},{10,9... | collective-permute-start | bytes 2150408 | tf_op jit(solution)/shard_map/ppermute | solution.py:35
  269.7 63.3 %collective-permute-start.2 = (bf16[1,320,1120]{2,1,0:T(8,128)(2,1)}, bf16[1,320,1120]{2,1,0:T(8,128)(2,1)}, u32[]{:S(2)}, u32[]{:S(2)}) collective-permute-start(bf16[1,320,1120]{2,1,0:T(8,128)(2,1)} %collective-permute-done), channel_id=1, source_target_pairs={{0,1},{1,2},{2,3},{3,0},{4,5},{5,6},{6,7},{7,4},{8,9},{9,10},{10,1... | collective-permute-start | bytes 2150408 | tf_op jit(solution)/shard_map/ppermute | solution.py:28
  365.1 1.6 copy-start.35
  375.2 97.2 %reduce-scatter.14.cloned.1.call-start = ((), (), s32[]{:S(2)}) async-start(), calls=%async_computation.17 | async-start | bytes 3686400 | tf_op jit(solution)/shard_map/reduce_scatter | solution.py:243
  386.1 557.4 %reduce-scatter.24.cloned.1.call-start = ((), (), s32[]{:S(2)}) async-start(), calls=%async_computation.24 | async-start | bytes 6451200
  434.3 42.6 %copy-start.6 = (bf16[1,4,320,5,56]{2,4,3,1,0:T(8,128)(2,1)S(1)}, bf16[1,4,320,5,56]{2,4,3,1,0:T(8,128)(2,1)}, u32[]{:S(2)}) copy-start(bf16[1,4,320,5,56]{2,4,3,1,0:T(8,128)(2,1)} %copy.103) | copy-start | bytes 2150404
  472.4 4.2 copy-start.10
  475.5 1.1 copy-start.4
  485.1 15.9 %all-to-all-start.4 = ((bf16[1,320,20,56]{1,3,0,2:T(8,128)(2,1)}), bf16[1,320,20,56]{1,3,0,2:T(8,128)(2,1)S(1)}, u32[]{:S(2)}, u32[]{:S(2)}) async-start(bf16[1,320,20,56]{1,3,0,2:T(8,128)(2,1)} %bitcast.51), calls=%async_computation.6 | async-start | bytes 1720320 | tf_op jit(solution)/shard_map/all_to_all | solution.py:281
  488.6 454.9 %reduce-scatter.18.cloned.1.call-start = ((), (), s32[]{:S(2)}) async-start(), calls=%async_computation.19 | async-start | bytes 19353600 | tf_op jit(solution)/shard_map/reduce_scatter | solution.py:291
  501.4 6.4 copy-start.15
  502.0 5.7 copy-start.12
  502.0 5.7 copy-start.20
  525.1 17.6 %copy-start.2 = (bf16[1,1280,5,3,56]{1,4,2,3,0:T(8,128)(2,1)S(1)}, bf16[1,1280,5,3,56]{1,4,2,3,0:T(8,128)(2,1)}, u32[]{:S(2)}) copy-start(bf16[1,1280,5,3,56]{1,4,2,3,0:T(8,128)(2,1)} %copy-done.1) | copy-start | bytes 6451204
  621.5 6.0 copy-start.8
  621.5 6.0 copy-start.13
  627.6 8.4 copy-start.21
  695.5 12.8 copy-start.23
  695.5 12.8 copy-start.25
  695.5 12.8 copy-start.27
  695.5 12.8 copy-start.29
  706.9 1.4 copy-start.3
  728.6 308.1 %reduce-scatter.22.cloned.1.call-start = ((), (), s32[]{:S(2)}) async-start(), calls=%async_computation.23 | async-start | bytes 7741440
  841.1 325.4 %reduce-scatter.20.cloned.1.call-start = ((), (), s32[]{:S(2)}) async-start(), calls=%async_computation.22 | async-start | bytes 7741440
  943.2 0.7 copy-start.34
  943.2 1.9 copy-start.32
  943.2 408.4 %all-reduce.8.cloned.1.call-start = ((), (), s32[]{:S(2)}) async-start(), calls=%async_computation.25 | async-start | bytes 10321920 | tf_op jit(solution)/shard_map/psum | solution.py:295
  949.0 7.7 copy-start.31
  949.0 8.5 copy-start.5
  949.0 8.5 copy-start.11
  1351.6 4.4 copy-start.18
Sparse Core Ops, SparseCore 0:
  9.6 57.3 all-gather.8
  68.5 34.0 all-gather.10
  104.8 57.7 all-gather.14
  164.7 56.1 all-gather.16
  222.8 41.0 all-gather.12
  375.3 56.9 reduce-scatter.15
  435.7 36.7 reduce-scatter.13
  480.9 50.8 reduce-scatter.23
  728.7 175.8 reduce-scatter.17
  908.5 128.1 reduce-scatter.21
  1040.8 125.5 reduce-scatter.19
  1170.4 181.1 all-reduce.7
